TPU v7x, 32 devices: a whole 2x2x4 slice. The times are simulated.
32 devices in a mesh: fsdp: 4 (over y, x), context: 4 (over z), tensor: 2 (over core).
Axes of the slice: x: 2, y: 2, z: 4, core: 2. Of those that a mesh axis runs over, the one named last changes fastest.
Arguments:
- tokens: bfloat16 [12288, 768], P(('fsdp', 'context')), may hold values from -6 to 6
- cotangent: bfloat16 [12288, 768], P(('fsdp', 'context')), may hold values from -6 to 6
- w_qkv: bfloat16 [3, 768, 768], P(None, 'fsdp', 'tensor'), may hold values from -0.21875 to 0.21875
- bias_qv: float32 [2, 768], P(None, 'tensor'), may hold values from -3 to 3
- w_attn_out: bfloat16 [768, 768], P('tensor', 'fsdp'), may hold values from -1.25 to 1.25
- w_up: bfloat16 [768, 3072], P('fsdp', 'tensor'), may hold values from -0.21875 to 0.21875
- bias_up: float32 [3072], P('tensor'), may hold values from -3 to 3
- w_down: bfloat16 [3072, 768], P('tensor', 'fsdp'), may hold values from -0.109375 to 0.109375
- gains: float32 [2, 768], replicated, may hold values from 0.1 to 1.9
- shifts: float32 [4, 768], replicated, may hold values from -3 to 3
- seq_lengths: int32 [4, 3], P('fsdp'), may hold values from 1 to 1536, 3072 in all within a row
- key_mask: int32 [12288], P('fsdp'), may hold values 0 or 1
Outputs:
- out: bfloat16 [12288, 768], P(('fsdp', 'context'))
- grad_tokens: bfloat16 [12288, 768], P(('fsdp', 'context'))
- grad_qkv: float32 [3, 768, 768], P(None, 'fsdp', 'tensor')
- grad_attn_out: float32 [768, 768], P('tensor', 'fsdp')
- grad_up: float32 [768, 3072], P('fsdp', 'tensor')
- grad_down: float32 [3072, 768], P('tensor', 'fsdp')
- grad_bias_qv: float32 [2, 768], P(None, 'tensor')
- grad_bias_up: float32 [3072], P('tensor')
- grad_gains: float32 [2, 768], replicated
- grad_shifts: float32 [4, 768], replicated
Inputs may be any that keep to these rules, and one draw needn't show every extreme that they name: `seq_lengths`: row f holds the lengths of the 3 sequences packed in order into the 3072 rows of group f; they sum to 3072 and the longest is 1536 in every row. `key_mask`: 1 marks a row that other rows of its sequence attend to; every row attends to itself.
All inputs are finite; a program needn't handle non-finite values. No bound on the sum of `key_mask` on one device may be relied on, other than what follows from the above.
Results may differ from a plain program's by a relative error of at most 0.022.
Values may be sent and summed in bfloat16 or wider, within the bound.
No kernel may reach another device: no remote copies, remote signals or barrier semaphores. Data moves between devices by JAX's collectives and lax.ppermute only.
A program may use at most 192 MiB of HBM per device.

v0:
```python
import jax
import jax.numpy as jnp
from jax import lax
from jax.sharding import PartitionSpec as P

EPSILON = 1e-12
SCORE_SCALE = 0.125
MASKED_SCORE = -1e30


def normalize(inputs):
    center = inputs - jnp.mean(inputs, axis=-1, keepdims=True)
    factor = lax.rsqrt(jnp.mean(center * center, axis=-1, keepdims=True) + EPSILON)
    return (center * factor, factor)


def norm_back(upstream, normed, factor, gain):
    scaled = upstream * gain
    return factor * (
        scaled
        - jnp.mean(scaled, axis=-1, keepdims=True)
        - normed * jnp.mean(scaled * normed, axis=-1, keepdims=True)
    )


def segment_ids(lengths_row, places):
    bounds = jnp.cumsum(lengths_row)
    return jnp.sum((places[:, None] >= bounds[None, :-1]).astype(jnp.int32), axis=1)


def split_heads(matrix, heads_here):
    return matrix.reshape(matrix.shape[0], heads_here, 64).transpose(1, 0, 2)


def join_heads(stacked):
    return stacked.transpose(1, 0, 2).reshape(stacked.shape[1], stacked.shape[0] * stacked.shape[2])


def score_grads(query_head, key_head, value_head, grad_head, log_head, delta_head, allowed):
    scores = (
        jnp.einsum("qd,kd->qk", query_head, key_head, preferred_element_type=jnp.float32)
        * SCORE_SCALE
    )
    probs = jnp.where(allowed, jnp.exp(scores - log_head[:, None]), 0.0)
    grad_prob = jnp.einsum("qd,kd->qk", grad_head, value_head, preferred_element_type=jnp.float32)
    grad_score = (probs * (grad_prob - delta_head[:, None])).astype(jnp.bfloat16)
    return (probs, grad_score)


def shards(
    tokens,
    cotangent,
    w_qkv,
    bias_qv,
    w_attn_out,
    w_up,
    bias_up,
    w_down,
    gains,
    shifts,
    seq_lengths,
    key_mask,
):
    row_count = tokens.shape[0]
    local_width = w_qkv.shape[2]
    heads_here = local_width // 64
    query_places = lax.axis_index("context") * row_count + jnp.arange(row_count, dtype=jnp.int32)
    lengths_row = seq_lengths[0]
    query_segment = segment_ids(lengths_row, query_places)

    def visible(length):
        key_places = jnp.arange(length, dtype=jnp.int32)
        key_segment = segment_ids(lengths_row, key_places)
        same = query_segment[:, None] == key_segment[None, :]
        return same & ((key_mask[None, :] == 1) | (query_places[:, None] == key_places[None, :]))

    w_proj, w_back, w_upper, w_lower = (
        lax.all_gather(w_qkv, "fsdp", axis=1, tiled=True),
        lax.all_gather(w_attn_out, "fsdp", axis=1, tiled=True),
        lax.all_gather(w_up, "fsdp", axis=0, tiled=True),
        lax.all_gather(w_down, "fsdp", axis=1, tiled=True),
    )
    projected = jnp.einsum("td,kde->kte", tokens, w_proj, preferred_element_type=jnp.float32)
    query = (projected[0] + bias_qv[0]).astype(jnp.bfloat16)
    key_rows = projected[1].astype(jnp.bfloat16)
    value_rows = (projected[2] + bias_qv[1]).astype(jnp.bfloat16)
    query_heads = split_heads(query, heads_here)
    start_state = (
        jnp.full((heads_here, row_count), MASKED_SCORE, jnp.float32),
        jnp.zeros((heads_here, row_count), jnp.float32),
        jnp.zeros((heads_here, row_count, 64), jnp.float32),
    )
    key_piece = lax.all_gather(key_rows, "context", axis=0, tiled=True)
    value_piece = lax.all_gather(value_rows, "context", axis=0, tiled=True)
    allowed = visible(key_piece.shape[0])

    def one_head(inputs):
        query_head, key_head, value_head, running_peak, running_total, running_sum = inputs
        scores = (
            jnp.einsum("qd,kd->qk", query_head, key_head, preferred_element_type=jnp.float32)
            * SCORE_SCALE
        )
        new_peak = jnp.maximum(
            running_peak, jnp.max(jnp.where(allowed, scores, MASKED_SCORE), axis=1)
        )
        weights = jnp.where(allowed, jnp.exp(scores - new_peak[:, None]), 0.0)
        fade = jnp.exp(running_peak - new_peak)
        new_total = running_total * fade + jnp.sum(weights, axis=1)
        new_sum = running_sum * fade[:, None] + jnp.dot(
            weights.astype(jnp.bfloat16), value_head, preferred_element_type=jnp.float32
        )
        return (new_peak, new_total, new_sum)

    peak, total, summed = lax.map(
        one_head,
        (
            query_heads,
            split_heads(key_piece, heads_here),
            split_heads(value_piece, heads_here),
            start_state[0],
            start_state[1],
            start_state[2],
        ),
    )
    attended = join_heads(summed / total[:, :, None]).astype(jnp.bfloat16)
    log_total = peak + jnp.log(total)
    branch_part = jnp.dot(attended, w_back, preferred_element_type=jnp.float32)
    first_sum = (
        tokens.astype(jnp.float32)
        + lax.psum(branch_part.astype(jnp.bfloat16), "tensor").astype(jnp.float32)
        + shifts[0]
    )
    normed1, factor1 = normalize(first_sum)
    first = normed1 * gains[0] + shifts[1]
    first_low = first.astype(jnp.bfloat16)
    upper = jnp.dot(first_low, w_upper, preferred_element_type=jnp.float32) + bias_up
    active_f, gelu_back = jax.vjp(lambda values: jax.nn.gelu(values, approximate=False), upper)
    active = active_f.astype(jnp.bfloat16)
    lower_part = jnp.dot(active, w_lower, preferred_element_type=jnp.float32)
    second_sum = (
        first + lax.psum(lower_part.astype(jnp.bfloat16), "tensor").astype(jnp.float32) + shifts[2]
    )
    normed2, factor2 = normalize(second_sum)
    out = (normed2 * gains[1] + shifts[3]).astype(jnp.bfloat16)
    upstream = cotangent.astype(jnp.float32)
    gain_two = jnp.sum(upstream * normed2, axis=0)
    shift_three = jnp.sum(upstream, axis=0)
    grad_second = norm_back(upstream, normed2, factor2, gains[1])
    shift_two = jnp.sum(grad_second, axis=0)
    lower_grad = grad_second.astype(jnp.bfloat16)
    grad_lower = jnp.einsum("tf,td->fd", active, lower_grad, preferred_element_type=jnp.float32)
    grad_active = jnp.einsum("td,fd->tf", lower_grad, w_lower, preferred_element_type=jnp.float32)
    grad_upper = gelu_back(grad_active)[0].astype(jnp.bfloat16)
    grad_bias_up = jnp.sum(grad_upper.astype(jnp.float32), axis=0)
    grad_upper_w = jnp.einsum(
        "td,tf->df", first_low, grad_upper, preferred_element_type=jnp.float32
    )
    back_part = jnp.einsum("tf,df->td", grad_upper, w_upper, preferred_element_type=jnp.float32)
    grad_first = grad_second + lax.psum(back_part.astype(jnp.bfloat16), "tensor").astype(
        jnp.float32
    )
    gain_one = jnp.sum(grad_first * normed1, axis=0)
    shift_one = jnp.sum(grad_first, axis=0)
    grad_first_sum = norm_back(grad_first, normed1, factor1, gains[0])
    shift_zero = jnp.sum(grad_first_sum, axis=0)
    branch_grad = grad_first_sum.astype(jnp.bfloat16)
    grad_back_w = jnp.einsum("te,td->ed", attended, branch_grad, preferred_element_type=jnp.float32)
    grad_attended = jnp.einsum(
        "td,ed->te", branch_grad, w_back, preferred_element_type=jnp.float32
    ).astype(jnp.bfloat16)
    grad_heads = split_heads(grad_attended, heads_here)
    delta = jnp.sum(
        grad_heads.astype(jnp.float32) * split_heads(attended, heads_here).astype(jnp.float32),
        axis=-1,
    )
    grad_query = jnp.zeros((heads_here, row_count, 64), jnp.float32)
    key_piece = lax.all_gather(key_rows, "context", axis=0, tiled=True)
    value_piece = lax.all_gather(value_rows, "context", axis=0, tiled=True)
    length = key_piece.shape[0]
    attend_allowed = visible(length)

    def one_head(inputs):
        query_head, key_head, value_head, grad_head, log_head, delta_head, grad_query_head = inputs
        probs, grad_score = score_grads(
            query_head, key_head, value_head, grad_head, log_head, delta_head, attend_allowed
        )
        grad_value = jnp.einsum(
            "qk,qd->kd", probs.astype(jnp.bfloat16), grad_head, preferred_element_type=jnp.float32
        )
        grad_query_head = (
            grad_query_head
            + jnp.einsum("qk,kd->qd", grad_score, key_head, preferred_element_type=jnp.float32)
            * SCORE_SCALE
        )
        grad_key = (
            jnp.einsum("qk,qd->kd", grad_score, query_head, preferred_element_type=jnp.float32)
            * SCORE_SCALE
        )
        return (grad_query_head, grad_key, grad_value)

    grad_query, key_terms, value_terms = lax.map(
        one_head,
        (
            query_heads,
            split_heads(key_piece, heads_here),
            split_heads(value_piece, heads_here),
            grad_heads,
            log_total,
            delta,
            grad_query,
        ),
    )
    grad_keys = join_heads(key_terms)
    grad_values = join_heads(value_terms)
    grad_keys_here, grad_values_here = (
        lax.psum_scatter(
            grad_keys.astype(jnp.bfloat16), "context", scatter_dimension=0, tiled=True
        ).astype(jnp.float32),
        lax.psum_scatter(
            grad_values.astype(jnp.bfloat16), "context", scatter_dimension=0, tiled=True
        ).astype(jnp.float32),
    )
    grad_query_low = join_heads(grad_query).astype(jnp.bfloat16)
    stacked = jnp.stack(
        [grad_query_low, grad_keys_here.astype(jnp.bfloat16), grad_values_here.astype(jnp.bfloat16)]
    )
    grad_proj = jnp.einsum("td,kte->kde", tokens, stacked, preferred_element_type=jnp.float32)
    grad_bias_qv = jnp.stack(
        [
            jnp.sum(stacked[0].astype(jnp.float32), axis=0),
            jnp.sum(stacked[2].astype(jnp.float32), axis=0),
        ]
    )
    input_part = jnp.einsum("kte,kde->td", stacked, w_proj, preferred_element_type=jnp.float32)
    grad_tokens = (
        grad_first_sum + lax.psum(input_part.astype(jnp.bfloat16), "tensor").astype(jnp.float32)
    ).astype(jnp.bfloat16)
    part_qkv, part_back, part_upper, part_lower = (
        lax.psum_scatter(
            grad_proj.astype(jnp.bfloat16), "fsdp", scatter_dimension=1, tiled=True
        ).astype(jnp.float32),
        lax.psum_scatter(
            grad_back_w.astype(jnp.bfloat16), "fsdp", scatter_dimension=1, tiled=True
        ).astype(jnp.float32),
        lax.psum_scatter(
            grad_upper_w.astype(jnp.bfloat16), "fsdp", scatter_dimension=0, tiled=True
        ).astype(jnp.float32),
        lax.psum_scatter(
            grad_lower.astype(jnp.bfloat16), "fsdp", scatter_dimension=1, tiled=True
        ).astype(jnp.float32),
    )
    share_qkv, share_back, share_upper, share_lower = (
        lax.psum(part_qkv.astype(jnp.bfloat16), "context").astype(jnp.float32),
        lax.psum(part_back.astype(jnp.bfloat16), "context").astype(jnp.float32),
        lax.psum(part_upper.astype(jnp.bfloat16), "context").astype(jnp.float32),
        lax.psum(part_lower.astype(jnp.bfloat16), "context").astype(jnp.float32),
    )
    gain_rows = jnp.stack([gain_one, gain_two])
    shift_rows = jnp.stack([shift_zero, shift_one, shift_two, shift_three])
    sum_bias_qv, sum_bias_up, sum_gains, sum_shifts = lax.psum(
        (grad_bias_qv, grad_bias_up, gain_rows, shift_rows), ("fsdp", "context")
    )
    return (
        out,
        grad_tokens,
        share_qkv,
        share_back,
        share_upper,
        share_lower,
        sum_bias_qv,
        sum_bias_up,
        sum_gains,
        sum_shifts,
    )


def solution(mesh):
    return jax.shard_map(
        shards,
        mesh=mesh,
        in_specs=(
            P(("fsdp", "context"), None),
            P(("fsdp", "context"), None),
            P(None, "fsdp", "tensor"),
            P(None, "tensor"),
            P("tensor", "fsdp"),
            P("fsdp", "tensor"),
            P("tensor"),
            P("tensor", "fsdp"),
            P(),
            P(),
            P("fsdp", None),
            P("fsdp"),
        ),
        out_specs=(
            P(("fsdp", "context"), None),
            P(("fsdp", "context"), None),
            P(None, "fsdp", "tensor"),
            P("tensor", "fsdp"),
            P("fsdp", "tensor"),
            P("tensor", "fsdp"),
            P(None, "tensor"),
            P("tensor"),
            P(),
            P(),
        ),
        check_vma=False,
    )
```

profile of v0, /device:TPU:0, one launch (start us, length us, event | category | flops | bytes accessed | tf_op | source)
XLA Modules:
  0.0 912.2 jit_solution(13213322940845944234)
XLA Ops:
  8.0 37.1 %all-gather.7.cloned.1.call-done = bf16[3,768,384]{2,1,0:T(8,128)(2,1)} async-done(((bf16[3,192,384]{2,1,0:T(8,128)(2,1)}), bf16[3,768,384]{2,1,0:T(8,128)(2,1)}) %all-gather.7.cloned.1.call-update) | async-done | bytes 1769488 | tf_op jit(solution)/shard_map/all_gather | solution.py:78
  54.5 10.9 %all_gather.23 = bf16[384,768]{0,1:T(8,128)(2,1)} all-gather(bf16[384,192]{0,1:T(8,128)(2,1)S(1)} %copy-done.28), channel_id=1, replica_groups=mesh['fsdp'=4,'context'=4,'tensor'=2] {'fsdp'}, dimensions={1}, use_global_device_ids=true | all-gather | bytes 737280 | tf_op jit(solution)/shard_map/all_gather | solution.py:79
  69.7 31.6 %all-gather.15.cloned.1.call-done = bf16[1,3072,384]{1,2,0:T(8,128)(2,1)} async-done(((bf16[1,768,384]{1,2,0:T(8,128)(2,1)}), bf16[1,3072,384]{1,2,0:T(8,128)(2,1)}) %all-gather.15.cloned.1.call-update) | async-done | bytes 2359312 | tf_op jit(solution)/shard_map/all_gather | solution.py:93
  101.3 5.7 copy.51
  107.0 45.2 %all-gather.9.cloned.1.call-done = bf16[3072,384]{0,1:T(8,128)(2,1)} async-done(((bf16[768,384]{0,1:T(8,128)(2,1)}), bf16[3072,384]{0,1:T(8,128)(2,1)}) %all-gather.9.cloned.1.call-update) | async-done | bytes 2359312 | tf_op jit(solution)/shard_map/all_gather | solution.py:94
  152.2 5.8 copy.52
  158.0 92.7 %while.32 = (s32[]{:T(128)}, f32[6,768]{1,0:T(8,128)S(1)}, f32[6,768]{1,0:T(8,128)S(1)}, f32[6,768,64]{1,2,0:T(8,128)S(1)}, bf16[6,768,64]{2,1,0:T(8,128)(2,1)},...) while((s32[]{:T(128)}, f32[6,768]{1,0:T(8,128)S(1)}, ...), condition=%wide.region_6.7_spmd.clone.clone, body=%wide.region_3.6_spmd.clone.sunk.clone | while | flops 658295808 | bytes 30400636 | solution.py:114
  158.1 5.0 select_reduce_fusion.3
  163.1 4.8 fusion.154
  167.9 5.4 fusion.155
  173.5 5.0 select_reduce_fusion.3
  183.4 5.4 fusion.155
  189.0 5.0 select_reduce_fusion.3
  194.0 4.8 fusion.154
  198.8 5.4 fusion.155
  204.4 5.0 select_reduce_fusion.3
  214.2 5.4 fusion.155
  219.8 5.0 select_reduce_fusion.3
  224.8 4.8 fusion.154
  229.7 5.4 fusion.155
  235.3 5.0 select_reduce_fusion.3
  245.1 5.4 fusion.155
  256.0 17.0 %all-reduce.8.cloned.1.call-done = bf16[768,768]{1,0:T(8,128)(2,1)} async-done(((bf16[768,768]{1,0:T(8,128)(2,1)}), bf16[768,768]{1,0:T(8,128)(2,1)}) %all-reduce.8.cloned.1.call-update) | async-done | bytes 1179664 | tf_op jit(solution)/shard_map/psum | solution.py:130
  275.5 37.7 %all-gather.11.cloned.1.call-done = bf16[768,1536]{1,0:T(8,128)(2,1)} async-done(((bf16[192,1536]{1,0:T(8,128)(2,1)}), bf16[768,1536]{1,0:T(8,128)(2,1)}) %all-gather.11.cloned.1.call-update) | async-done | bytes 2359312 | tf_op jit(solution)/shard_map/all_gather | solution.py:80
  313.3 15.5 %multiply_convert_fusion.1 = (bf16[768,1536]{1,0:T(8,128)(2,1)}, f32[768,1536]{1,0:T(8,128)}, f32[768,1536]{1,0:T(8,128)}) fusion(f32[1536]{0:T(1024)S(1)} %copy-done.48, bf16[768,1536]{1,0:T(8,128)(2,1)} %all-gather.11.cloned.1.call-done, f32[768]{0:T(1024)S(1)} %get-tuple-element.273, f32[768]{0:T(1024)S(1)} %get-tuple-element.277, ...), kind=kOutput, calls=%fused_computation.67 | convolution fusion | flops 1895104512 | bytes 16536576 | tf_op jit(solution)/shard_map/dot_general | solution.py:136
  328.7 23.6 %all-gather.13.cloned.1.call-done = bf16[1536,768]{0,1:T(8,128)(2,1)} async-done(((bf16[1536,192]{0,1:T(8,128)(2,1)}), bf16[1536,768]{0,1:T(8,128)(2,1)}) %all-gather.13.cloned.1.call-update) | async-done | bytes 2359312 | tf_op jit(solution)/shard_map/all_gather | solution.py:81
  352.3 5.4 convolution_convert_fusion.4
  357.8 19.8 %all-reduce.10.cloned.1.call-done = bf16[768,768]{1,0:T(8,128)(2,1)} async-done(((bf16[768,768]{1,0:T(8,128)(2,1)}), bf16[768,768]{1,0:T(8,128)(2,1)}) %all-reduce.10.cloned.1.call-update) | async-done | bytes 1179664 | tf_op jit(solution)/shard_map/psum | solution.py:141
  384.8 7.2 convert_reduce_fusion
  398.5 19.1 %all-reduce.12.cloned.1.call-done = bf16[768,768]{1,0:T(8,128)(2,1)} async-done(((bf16[768,768]{1,0:T(8,128)(2,1)}), bf16[768,768]{1,0:T(8,128)(2,1)}) %all-reduce.12.cloned.1.call-update) | async-done | bytes 1179664 | tf_op jit(solution)/shard_map/psum | solution.py:159
  426.4 106.2 %while.33 = (s32[]{:T(128)}, bf16[6,768,64]{1,2,0:T(8,128)(2,1)}, bf16[6,3072,64]{1,2,0:T(8,128)(2,1)}, bf16[6,3072,64]{1,2,0:T(8,128)(2,1)}, bf16[6,768,64]{2,1...) while((s32[]{:T(128)}, bf16[6,768,64]{1,2,0:T(8,128)(2,1)}, ...), condition=%wide.region_20.21_spmd.clone.clone, body=%wide.region_19.20_spmd.clone.sunk.clone | while | flops 1536147456 | bytes 51950792 | solution.py:201
  427.2 5.4 exponential_select_fusion.4
  444.9 5.4 exponential_select_fusion.4
  462.6 5.4 exponential_select_fusion.4
  480.3 5.4 exponential_select_fusion.4
  498.0 5.4 exponential_select_fusion.4
  515.7 5.4 exponential_select_fusion.4
  543.6 42.3 %reduce-scatter.9.cloned.1.call-done = bf16[768,384]{1,0:T(8,128)(2,1)} async-done(((bf16[3072,384]{1,0:T(8,128)(2,1)}), bf16[768,384]{1,0:T(8,128)(2,1)}) %reduce-scatter.9.cloned.1.call-update) | async-done | bytes 589840 | tf_op jit(solution)/shard_map/reduce_scatter | solution.py:216
  586.0 49.3 %reduce-scatter.11.cloned.1.call-done = bf16[768,384]{1,0:T(8,128)(2,1)} async-done(((bf16[3072,384]{1,0:T(8,128)(2,1)}), bf16[768,384]{1,0:T(8,128)(2,1)}) %reduce-scatter.11.cloned.1.call-update) | async-done | bytes 589840 | tf_op jit(solution)/shard_map/reduce_scatter | solution.py:219
  639.5 5.2 copy.60
  650.7 5.9 convolution_convert_fusion
  657.4 5.9 convolution_convert_fusion.1
  669.1 10.8 %reduce-scatter.19.cloned.1.call-done = bf16[192,1152]{1,0:T(8,128)(2,1)} async-done(((bf16[768,1152]{1,0:T(8,128)(2,1)}), bf16[192,1152]{1,0:T(8,128)(2,1)}) %reduce-scatter.19.cloned.1.call-update) | async-done | bytes 442384
  682.6 26.1 %reduce-scatter.13.cloned.1.call-done = bf16[384,192]{0,1:T(8,128)(2,1)} async-done(((bf16[384,768]{0,1:T(8,128)(2,1)}), bf16[384,192]{0,1:T(8,128)(2,1)}) %reduce-scatter.13.cloned.1.call-update) | async-done | bytes 147472 | tf_op jit(solution)/shard_map/reduce_scatter | solution.py:242
  708.7 40.4 %reduce-scatter.17.cloned.1.call-done = bf16[1536,192]{0,1:T(8,128)(2,1)} async-done(((bf16[1536,768]{0,1:T(8,128)(2,1)}), bf16[1536,192]{0,1:T(8,128)(2,1)}) %reduce-scatter.17.cloned.1.call-update) | async-done | bytes 589840 | tf_op jit(solution)/shard_map/reduce_scatter | solution.py:248
  749.1 40.3 %reduce-scatter.15.cloned.1.call-done = bf16[192,1536]{1,0:T(8,128)(2,1)} async-done(((bf16[768,1536]{1,0:T(8,128)(2,1)}), bf16[192,1536]{1,0:T(8,128)(2,1)}) %reduce-scatter.15.cloned.1.call-update) | async-done | bytes 589840 | tf_op jit(solution)/shard_map/reduce_scatter | solution.py:245
  795.0 79.4 %all-reduce = (f32[2,384]{1,0:T(2,128)}, f32[1536]{0:T(1024)}, f32[2,768]{1,0:T(2,128)}, f32[4,768]{1,0:T(4,128)}) all-reduce(f32[2,384]{1,0:T(2,128)S(1)} %pad_maximum_fusion.5, f32[1536]{0:T(1024)} %get-tuple-element.353, f32[2,768]{1,0:T(2,128)S(1)} %pad_maximum_fusion.4, ...), channel_id=1, replica_groups=mesh['fsdp'=4,'context'=4,'tensor'=2] {'fsdp','context'}, use_global_device_ids=true, to_apply=%region_34.35 | all-reduce | flops 6912 | bytes 55296 | tf_op jit(solution)/shard_map/psum | solution.py:260
  877.0 21.2 %all-reduce.16.cloned.1.call-done = (bf16[3,192,384]{1,2,0:T(8,128)(2,1)}, bf16[384,192]{0,1:T(8,128)(2,1)}, bf16[192,1536]{1,0:T(8,128)(2,1)}, bf16[1536,192]{0,1:T(8,128)(2,1)}) async-done(((bf16[3,192,384]{1,2,0:T(8,128)(2,1)}, bf16[384,192]{0,1:T(8,128)(2,1)}, bf16[192,1536]{1,0:T(8,128)(2,1)}, bf16[1536,192]{0,1:T(8,128)(2,1)}), (bf16[3,192,384]{1,2,0:T(8,128)(2,1)}, bf16[384,192]{0,1:T(8,128)(2,1)}, ...) | async-done | bytes 1769488 | tf_op jit(solution)/shard_map/psum | solution.py:253
  (289 shorter events, 179.6 us)
Async XLA Ops:
  7.2 37.9 %all-gather.7.cloned.1.call-start = ((), (), s32[]{:S(2)}) async-start(), calls=%async_computation.6 | async-start | bytes 2211840 | tf_op jit(solution)/shard_map/all_gather | solution.py:78
  7.9 43.3 %copy-start.45 = (f32[2,384]{1,0:T(2,128)S(1)}, f32[2,384]{1,0:T(2,128)}, u32[]{:S(2)}) copy-start(f32[2,384]{1,0:T(2,128)} %param.19) | copy-start | bytes 9220
  7.9 93.3 %all-gather.15.cloned.1.call-start = ((), (), s32[]{:S(2)}) async-start(), calls=%async_computation.19 | async-start | bytes 2949120 | tf_op jit(solution)/shard_map/all_gather | solution.py:93
  50.2 3.4 copy-start.49
  50.2 4.3 copy-start.28
  50.2 15.9 %copy-start.43 = (s32[3072]{0:T(1024)S(1)}, s32[3072]{0:T(1024)}, u32[]{:S(2)}) copy-start(s32[3072]{0:T(1024)} %param.27) | copy-start | bytes 36868
  51.1 101.1 %all-gather.9.cloned.1.call-start = ((), (), s32[]{:S(2)}) async-start(), calls=%async_computation.7 | async-start | bytes 2949120 | tf_op jit(solution)/shard_map/all_gather | solution.py:94
  51.2 15.6 %slice-start = ((f32[3,768,384]{1,2,0:T(8,128)}), f32[1,768,384]{1,2,0:T(8,128)S(1)}, s32[]{:S(2)}) async-start(f32[3,768,384]{1,2,0:T(8,128)} %copy-done.13), calls=%async_computation.22 | async-start | bytes 2359296 | tf_op jit(solution)/shard_map/slice | solution.py:84
  53.6 219.4 %all-reduce.8.cloned.1.call-start = ((), (), s32[]{:S(2)}) async-start(), calls=%async_computation.8 | async-start | bytes 2359296 | tf_op jit(solution)/shard_map/psum | solution.py:130
  152.2 5.8 copy-start.14
  152.2 5.8 copy-start.22
  152.2 5.8 copy-start.25
  152.2 5.8 copy-start.29
  152.2 5.8 copy-start.36
  158.0 94.5 %copy-start.7 = (bf16[384,768]{0,1:T(8,128)(2,1)S(1)}, bf16[384,768]{0,1:T(8,128)(2,1)}, u32[]{:S(2)}) copy-start(bf16[384,768]{0,1:T(8,128)(2,1)} %all_gather.23) | copy-start | bytes 1769476
  250.7 147.1 %copy-start.23 = (f32[6,768]{1,0:T(8,128)}, f32[6,768]{1,0:T(8,128)S(1)}, u32[]{:S(2)}) copy-start(f32[6,768]{1,0:T(8,128)S(1)} %get-tuple-element.114) | copy-start | bytes 55300
  252.6 3.3 copy-start.42
  252.6 20.4 %copy-start = (bf16[768,768]{1,0:T(8,128)(2,1)S(1)}, bf16[768,768]{1,0:T(8,128)(2,1)}, u32[]{:S(2)}) copy-start(bf16[768,768]{1,0:T(8,128)(2,1)} %param.16) | copy-start | bytes 3538948
  254.4 58.8 %all-gather.11.cloned.1.call-start = ((), (), s32[]{:S(2)}) async-start(), calls=%async_computation.9 | async-start | bytes 2949120 | tf_op jit(solution)/shard_map/all_gather | solution.py:80
  255.0 97.3 %all-gather.13.cloned.1.call-start = ((), (), s32[]{:S(2)}) async-start(), calls=%async_computation.10 | async-start | bytes 2949120 | tf_op jit(solution)/shard_map/all_gather | solution.py:81
  255.6 122.0 %all-reduce.10.cloned.1.call-start = ((), (), s32[]{:S(2)}) async-start(), calls=%async_computation.11 | async-start | bytes 2359296 | tf_op jit(solution)/shard_map/psum | solution.py:141
  255.9 161.6 %copy-start.32 = (f32[768]{0:T(1024)}, f32[768]{0:T(1024)S(1)}, u32[]{:S(2)}) copy-start(f32[768]{0:T(1024)S(1)} %get-tuple-element.277) | copy-start | bytes 9220
  256.0 121.6 %copy-start.37 = (f32[768]{0:T(1024)}, f32[768]{0:T(1024)S(1)}, u32[]{:S(2)}) copy-start(f32[768]{0:T(1024)S(1)} %get-tuple-element.273) | copy-start | bytes 9220
  256.0 161.6 %copy-start.26 = (f32[768]{0:T(1024)}, f32[768]{0:T(1024)S(1)}, u32[]{:S(2)}) copy-start(f32[768]{0:T(1024)S(1)} %get-tuple-element.274) | copy-start | bytes 9220
  273.0 40.3 %copy-start.48 = (f32[1536]{0:T(1024)S(1)}, f32[1536]{0:T(1024)}, u32[]{:S(2)}) copy-start(f32[1536]{0:T(1024)} %param.22) | copy-start | bytes 18436
  274.9 142.7 %copy-start.30 = (f32[768]{0:T(1024)}, f32[768]{0:T(1024)S(1)}, u32[]{:S(2)}) copy-start(f32[768]{0:T(1024)S(1)} %broadcast_multiply_fusion.5) | copy-start | bytes 9220
  275.5 142.0 %copy-start.34 = (f32[768]{0:T(1024)}, f32[768]{0:T(1024)S(1)}, u32[]{:S(2)}) copy-start(f32[768]{0:T(1024)S(1)} %add_rsqrt_fusion.1) | copy-start | bytes 9220
  357.8 59.8 %all-reduce.12.cloned.1.call-start = ((), (), s32[]{:S(2)}) async-start(), calls=%async_computation.12 | async-start | bytes 2359296 | tf_op jit(solution)/shard_map/psum | solution.py:159
  384.8 7.3 copy-start.3
  384.8 8.6 copy-start.46
  396.5 189.5 %reduce-scatter.9.cloned.1.call-start = ((), (), s32[]{:S(2)}) async-start(), calls=%async_computation.13 | async-start | bytes 2949120 | tf_op jit(solution)/shard_map/reduce_scatter | solution.py:216
  417.6 4.0 copy-start.2
  417.6 4.0 copy-start.4
  417.6 4.0 copy-start.12
  537.0 98.3 %reduce-scatter.11.cloned.1.call-start = ((), (), s32[]{:S(2)}) async-start(), calls=%async_computation.14 | async-start | bytes 2949120 | tf_op jit(solution)/shard_map/reduce_scatter | solution.py:219
  541.3 138.6 %reduce-scatter.19.cloned.1.call-start = ((), (), s32[]{:S(2)}) async-start(), calls=%async_computation.20 | async-start | bytes 2211840
  647.9 60.8 %reduce-scatter.13.cloned.1.call-start = ((), (), s32[]{:S(2)}) async-start(), calls=%async_computation.16 | async-start | bytes 737280 | tf_op jit(solution)/shard_map/reduce_scatter | solution.py:242
  650.7 98.4 %reduce-scatter.17.cloned.1.call-start = ((), (), s32[]{:S(2)}) async-start(), calls=%async_computation.18 | async-start | bytes 2949120 | tf_op jit(solution)/shard_map/reduce_scatter | solution.py:248
  656.7 132.8 %reduce-scatter.15.cloned.1.call-start = ((), (), s32[]{:S(2)}) async-start(), calls=%async_computation.17 | async-start | bytes 2949120 | tf_op jit(solution)/shard_map/reduce_scatter | solution.py:245
  663.3 211.1 %all-reduce.14.cloned.1.call-start = ((), (), s32[]{:S(2)}) async-start(), calls=%async_computation.15 | async-start | bytes 2359296 | tf_op jit(solution)/shard_map/psum | solution.py:236
  669.0 123.0 %copy-start.40 = (f32[768]{0:T(1024)S(1)}, f32[768]{0:T(1024)}, u32[]{:S(2)}) copy-start(f32[768]{0:T(1024)} %get-tuple-element.263) | copy-start | bytes 9220
  669.0 123.6 %copy-start.39 = (f32[768]{0:T(1024)S(1)}, f32[768]{0:T(1024)}, u32[]{:S(2)}) copy-start(f32[768]{0:T(1024)} %get-tuple-element.268) | copy-start | bytes 9220
  669.0 123.6 %copy-start.38 = (f32[768]{0:T(1024)S(1)}, f32[768]{0:T(1024)}, u32[]{:S(2)}) copy-start(f32[768]{0:T(1024)} %get-tuple-element.269) | copy-start | bytes 9220
  669.0 123.6 %copy-start.41 = (f32[768]{0:T(1024)S(1)}, f32[768]{0:T(1024)}, u32[]{:S(2)}) copy-start(f32[768]{0:T(1024)} %get-tuple-element.338) | copy-start | bytes 9220
  669.0 124.2 %copy-start.11 = (bf16[6,768,64]{1,2,0:T(8,128)(2,1)S(1)}, bf16[6,768,64]{1,2,0:T(8,128)(2,1)}, u32[]{:S(2)}) copy-start(bf16[6,768,64]{1,2,0:T(8,128)(2,1)} %get-tuple-element.116) | copy-start | bytes 1769476
  669.0 229.1 %all-reduce.16.cloned.1.call-start = ((), (), s32[]{:S(2)}) async-start(), calls=%async_computation.21 | async-start | bytes 3833856 | tf_op jit(solution)/shard_map/psum | solution.py:253
  682.6 112.2 %copy-start.20 = (bf16[768,384]{1,0:T(8,128)(2,1)S(1)}, bf16[768,384]{1,0:T(8,128)(2,1)}, u32[]{:S(2)}) copy-start(bf16[768,384]{1,0:T(8,128)(2,1)} %reduce-scatter.11.cloned.1.call-done) | copy-start | bytes 1769476
  898.2 6.1 copy-start.18
  (30 other events, 62.3 us)
Sparse Core Ops, SparseCore 0:
  9.8 35.1 all-gather.6
  51.2 49.9 all-gather.14
  103.4 48.7 all-gather.8
  254.5 18.4 all-reduce.7
  274.7 38.5 all-gather.10
  315.0 37.3 all-gather.12
  357.9 19.6 all-reduce.9
  396.6 20.8 all-reduce.11
  537.1 48.8 reduce-scatter.8
  588.1 47.1 reduce-scatter.10
  648.0 31.8 reduce-scatter.18
  683.2 25.4 reduce-scatter.12
  711.7 37.3 reduce-scatter.16
  752.0 37.3 reduce-scatter.14
  792.2 19.6 all-reduce.13
  815.0 83.1 all-reduce.15
where the time goes:
time: 918 us; the launch traced here: 912 us
  waiting for transfers between devices  464 us (51%)
  matrix products  224 us (24%)
  blocking collectives  90.3 us (10%)
  other arithmetic  62 us (7%)
  local copies, waits for them, and re-layouts  56 us (6%)
  between operations  14.7 us (2%)
    psum x1, blocking collectives, shards(): lax.psum((grad_bias_qv, grad_bias_up, gain_rows, shift_rows), ('fsdp', 'c...  79.4 us
    reduce_scatter x1, waiting for transfers between devices, shards(): lax.psum_scatter(grad_values.astype(jnp.bfloat16), 'context', scatter_dim...  49.3 us
    all_gather x1, waiting for transfers between devices, shards(): value_piece = lax.all_gather(value_rows, 'context', axis=0, tiled=True)  45.2 us
    reduce_scatter x1, waiting for transfers between devices, shards(): lax.psum_scatter(grad_keys.astype(jnp.bfloat16), 'context', scatter_dimen...  42.3 us
    reduce_scatter x1, waiting for transfers between devices, shards(): lax.psum_scatter(grad_lower.astype(jnp.bfloat16), 'fsdp', scatter_dimensi...  40.4 us
    reduce_scatter x1, waiting for transfers between devices, shards(): lax.psum_scatter(grad_upper_w.astype(jnp.bfloat16), 'fsdp', scatter_dimen...  40.3 us
    all_gather x1, waiting for transfers between devices, shards(): lax.all_gather(w_up, 'fsdp', axis=0, tiled=True)  37.7 us
    all_gather x1, waiting for transfers between devices, shards(): lax.all_gather(w_qkv, 'fsdp', axis=1, tiled=True)  37.1 us
  transfers between devices with their start and end apart: 16, of which 15 were waited for; matrix products, arithmetic and copies ran while one was open for 8% of the time, Pallas kernels for 0%

commit v1 on v0

--- a/solution.py
+++ b/solution.py
@@ -90,8 +90,13 @@
         jnp.zeros((heads_here, row_count), jnp.float32),
         jnp.zeros((heads_here, row_count, 64), jnp.float32),
     )
-    key_piece = lax.all_gather(key_rows, "context", axis=0, tiled=True)
-    value_piece = lax.all_gather(value_rows, "context", axis=0, tiled=True)
+    key_piece, value_piece = jnp.split(
+        lax.all_gather(
+            jnp.concatenate([key_rows, value_rows], axis=1), "context", axis=0, tiled=True
+        ),
+        [key_rows.shape[1]],
+        axis=1,
+    )
     allowed = visible(key_piece.shape[0])
 
     def one_head(inputs):

time: 918 us -> 1020 us (1.11)
  waiting for transfers between devices: 464 us -> 529 us
  local copies, waits for them, and re-layouts: 56 us -> 89.3 us
    all_gather x0 -> x1, waiting for transfers between devices: none -> 71.5 us  [shards(): lax.all_gather(jnp.concatenate([key_rows, value_rows], axis=1), 'context'...]
    dynamic_update_slice x12, local copies, waits for them, and re-layouts: 1.03 us -> 16.3 us  [shards(): lax.map(one_head, (query_heads, split_heads(key_piece, heads_here), split...]
    reshape x2 -> x4, local copies, waits for them, and re-layouts: 11.5 us -> 21.3 us  [split_heads(): return matrix.reshape(matrix.shape[0], heads_here, 64).transpose(1, 0, 2)]
    unnamed x103 -> x97, local copies, waits for them, and re-layouts: 21.6 us -> 20.8 us
  transfers between devices with their start and end apart: 16 -> 17, of which waited for: 15 -> 16; matrix products, arithmetic and copies ran while one was open for 8% -> 9% of each run, Pallas kernels for 0% -> 0%
where the time goes in v1:
time: 1020 us; the launch traced here: 1010 us
  waiting for transfers between devices  529 us (52%)
  matrix products  223 us (22%)
  blocking collectives  90.3 us (9%)
  local copies, waits for them, and re-layouts  89.3 us (9%)
  other arithmetic  61.1 us (6%)
  between operations  14.8 us (1%)
    psum x1, blocking collectives, shards(): lax.psum((grad_bias_qv, grad_bias_up, gain_rows, shift_rows), ('fsdp', 'c...  79.4 us
    all_gather x1, waiting for transfers between devices, shards(): lax.all_gather(jnp.concatenate([key_rows, value_rows], axis=1), 'context'...  71.5 us
    reduce_scatter x1, waiting for transfers between devices, shards(): lax.psum_scatter(grad_values.astype(jnp.bfloat16), 'context', scatter_dim...  49.4 us
    all_gather x1, waiting for transfers between devices, shards(): value_piece = lax.all_gather(value_rows, 'context', axis=0, tiled=True)  44.5 us
    reduce_scatter x1, waiting for transfers between devices, shards(): lax.psum_scatter(grad_keys.astype(jnp.bfloat16), 'context', scatter_dimen...  42.5 us
    reduce_scatter x1, waiting for transfers between devices, shards(): lax.psum_scatter(grad_upper_w.astype(jnp.bfloat16), 'fsdp', scatter_dimen...  40.3 us
    reduce_scatter x1, waiting for transfers between devices, shards(): lax.psum_scatter(grad_lower.astype(jnp.bfloat16), 'fsdp', scatter_dimensi...  40.3 us
    all_gather x1, waiting for transfers between devices, shards(): lax.all_gather(w_up, 'fsdp', axis=0, tiled=True)  37.7 us
  transfers between devices with their start and end apart: 17, of which 16 were waited for; matrix products, arithmetic and copies ran while one was open for 9% of the time, Pallas kernels for 0%

profile of v1, /device:TPU:0, one launch (start us, length us, event | category | flops | bytes accessed | tf_op | source)
XLA Modules:
  0.0 1009.0 jit_solution(2827400862535599114)
XLA Ops:
  8.7 36.3 %all-gather.8.cloned.1.call-done = bf16[3,768,384]{2,1,0:T(8,128)(2,1)} async-done(((bf16[3,192,384]{2,1,0:T(8,128)(2,1)}), bf16[3,768,384]{2,1,0:T(8,128)(2,1)}) %all-gather.8.cloned.1.call-update) | async-done | bytes 1769488 | tf_op jit(solution)/shard_map/all_gather | solution.py:78
  52.0 10.9 %all_gather.23 = bf16[384,768]{0,1:T(8,128)(2,1)} all-gather(bf16[384,192]{0,1:T(8,128)(2,1)S(1)} %copy-done.28), channel_id=1, replica_groups=mesh['fsdp'=4,'context'=4,'tensor'=2] {'fsdp'}, dimensions={1}, use_global_device_ids=true | all-gather | bytes 737280 | tf_op jit(solution)/shard_map/all_gather | solution.py:79
  69.6 71.5 %all-gather.10.cloned.1.call-done = bf16[3072,768]{0,1:T(8,128)(2,1)} async-done(((bf16[768,768]{0,1:T(8,128)(2,1)}), bf16[3072,768]{0,1:T(8,128)(2,1)}) %all-gather.10.cloned.1.call-update) | async-done | bytes 4718608 | tf_op jit(solution)/shard_map/all_gather | solution.py:94
  145.3 5.7 copy.57
  155.1 107.9 %while.32 = (s32[]{:T(128)}, f32[6,768]{1,0:T(8,128)}, f32[6,768]{1,0:T(8,128)}, f32[6,768,64]{1,2,0:T(8,128)S(1)}, bf16[6,768,64]{2,1,0:T(8,128)(2,1)}, /*index...) while((s32[]{:T(128)}, f32[6,768]{1,0:T(8,128)}, ...), condition=%wide.region_6.7_spmd.clone.clone, body=%wide.region_3.6_spmd.clone.sunk.clone | while | flops 658295808 | bytes 30426292 | solution.py:119
  155.1 5.0 select_reduce_fusion.3
  160.1 4.8 fusion.155
  164.9 5.4 fusion.156
  173.1 4.9 select_reduce_fusion.3
  182.9 5.4 fusion.156
  191.0 4.9 select_reduce_fusion.3
  200.8 5.4 fusion.156
  208.9 4.9 select_reduce_fusion.3
  218.7 5.4 fusion.156
  226.8 4.9 select_reduce_fusion.3
  236.6 5.4 fusion.156
  244.7 4.9 select_reduce_fusion.3
  254.5 5.4 fusion.156
  268.0 16.9 %all-reduce.8.cloned.1.call-done = bf16[768,768]{1,0:T(8,128)(2,1)} async-done(((bf16[768,768]{1,0:T(8,128)(2,1)}), bf16[768,768]{1,0:T(8,128)(2,1)}) %all-reduce.8.cloned.1.call-update) | async-done | bytes 1179664 | tf_op jit(solution)/shard_map/psum | solution.py:135
  287.4 37.7 %all-gather.12.cloned.1.call-done = bf16[768,1536]{1,0:T(8,128)(2,1)} async-done(((bf16[192,1536]{1,0:T(8,128)(2,1)}), bf16[768,1536]{1,0:T(8,128)(2,1)}) %all-gather.12.cloned.1.call-update) | async-done | bytes 2359312 | tf_op jit(solution)/shard_map/all_gather | solution.py:80
  325.2 15.5 %multiply_convert_fusion.1 = (bf16[768,1536]{1,0:T(8,128)(2,1)}, f32[768,1536]{1,0:T(8,128)}, f32[768,1536]{1,0:T(8,128)}) fusion(f32[1536]{0:T(1024)S(1)} %copy-done.47, bf16[768,1536]{1,0:T(8,128)(2,1)} %all-gather.12.cloned.1.call-done, f32[768]{0:T(1024)S(1)} %get-tuple-element.273, f32[768]{0:T(1024)S(1)} %get-tuple-element.277, ...), kind=kOutput, calls=%fused_computation.67 | convolution fusion | flops 1895104512 | bytes 16536576 | tf_op jit(solution)/shard_map/dot_general | solution.py:141
  340.6 23.6 %all-gather.14.cloned.1.call-done = bf16[1536,768]{0,1:T(8,128)(2,1)} async-done(((bf16[1536,192]{0,1:T(8,128)(2,1)}), bf16[1536,768]{0,1:T(8,128)(2,1)}) %all-gather.14.cloned.1.call-update) | async-done | bytes 2359312 | tf_op jit(solution)/shard_map/all_gather | solution.py:81
  364.2 5.4 convolution_convert_fusion.4
  372.7 16.8 %all-reduce.10.cloned.1.call-done = bf16[768,768]{1,0:T(8,128)(2,1)} async-done(((bf16[768,768]{1,0:T(8,128)(2,1)}), bf16[768,768]{1,0:T(8,128)(2,1)}) %all-reduce.10.cloned.1.call-update) | async-done | bytes 1179664 | tf_op jit(solution)/shard_map/psum | solution.py:146
  396.7 7.5 convert_reduce_fusion
  409.6 32.6 %all-gather.18.cloned.1.call-done = bf16[1,3072,384]{1,2,0:T(8,128)(2,1)} async-done(((bf16[1,768,384]{1,2,0:T(8,128)(2,1)}), bf16[1,3072,384]{1,2,0:T(8,128)(2,1)}) %all-gather.18.cloned.1.call-update) | async-done | bytes 2359312 | tf_op jit(solution)/shard_map/all_gather | solution.py:182
  442.2 5.9 copy.59
  448.1 44.5 %all-gather.16.cloned.1.call-done = bf16[3072,384]{0,1:T(8,128)(2,1)} async-done(((bf16[768,384]{0,1:T(8,128)(2,1)}), bf16[3072,384]{0,1:T(8,128)(2,1)}) %all-gather.16.cloned.1.call-update) | async-done | bytes 2359312 | tf_op jit(solution)/shard_map/all_gather | solution.py:183
  492.6 5.7 copy.60
  498.9 15.0 %all-reduce.12.cloned.1.call-done = bf16[768,768]{1,0:T(8,128)(2,1)} async-done(((bf16[768,768]{1,0:T(8,128)(2,1)}), bf16[768,768]{1,0:T(8,128)(2,1)}) %all-reduce.12.cloned.1.call-update) | async-done | bytes 1179664 | tf_op jit(solution)/shard_map/psum | solution.py:164
  522.9 106.1 %while.33 = (s32[]{:T(128)}, bf16[6,768,64]{1,2,0:T(8,128)(2,1)}, bf16[6,3072,64]{1,2,0:T(8,128)(2,1)}, bf16[6,3072,64]{1,2,0:T(8,128)(2,1)}, bf16[6,768,64]{2,1...) while((s32[]{:T(128)}, bf16[6,768,64]{1,2,0:T(8,128)(2,1)}, ...), condition=%wide.region_20.21_spmd.clone.clone, body=%wide.region_19.20_spmd.clone.sunk.clone | while | flops 1536147456 | bytes 51950792 | solution.py:206
  523.6 5.4 exponential_select_fusion.4
  541.3 5.4 exponential_select_fusion.4
  559.0 5.4 exponential_select_fusion.4
  576.7 5.4 exponential_select_fusion.4
  594.4 5.4 exponential_select_fusion.4
  612.1 5.4 exponential_select_fusion.4
  640.0 42.5 %reduce-scatter.9.cloned.1.call-done = bf16[768,384]{1,0:T(8,128)(2,1)} async-done(((bf16[3072,384]{1,0:T(8,128)(2,1)}), bf16[768,384]{1,0:T(8,128)(2,1)}) %reduce-scatter.9.cloned.1.call-update) | async-done | bytes 589840 | tf_op jit(solution)/shard_map/reduce_scatter | solution.py:221
  682.5 49.4 %reduce-scatter.11.cloned.1.call-done = bf16[768,384]{1,0:T(8,128)(2,1)} async-done(((bf16[3072,384]{1,0:T(8,128)(2,1)}), bf16[768,384]{1,0:T(8,128)(2,1)}) %reduce-scatter.11.cloned.1.call-update) | async-done | bytes 589840 | tf_op jit(solution)/shard_map/reduce_scatter | solution.py:224
  736.2 5.2 copy.68
  747.4 5.8 convolution_convert_fusion
  754.0 5.9 convolution_convert_fusion.1
  765.7 10.9 %reduce-scatter.19.cloned.1.call-done = bf16[192,1152]{1,0:T(8,128)(2,1)} async-done(((bf16[768,1152]{1,0:T(8,128)(2,1)}), bf16[192,1152]{1,0:T(8,128)(2,1)}) %reduce-scatter.19.cloned.1.call-update) | async-done | bytes 442384
  779.3 26.2 %reduce-scatter.13.cloned.1.call-done = bf16[384,192]{0,1:T(8,128)(2,1)} async-done(((bf16[384,768]{0,1:T(8,128)(2,1)}), bf16[384,192]{0,1:T(8,128)(2,1)}) %reduce-scatter.13.cloned.1.call-update) | async-done | bytes 147472 | tf_op jit(solution)/shard_map/reduce_scatter | solution.py:247
  805.5 40.3 %reduce-scatter.17.cloned.1.call-done = bf16[1536,192]{0,1:T(8,128)(2,1)} async-done(((bf16[1536,768]{0,1:T(8,128)(2,1)}), bf16[1536,192]{0,1:T(8,128)(2,1)}) %reduce-scatter.17.cloned.1.call-update) | async-done | bytes 589840 | tf_op jit(solution)/shard_map/reduce_scatter | solution.py:253
  845.8 40.3 %reduce-scatter.15.cloned.1.call-done = bf16[192,1536]{1,0:T(8,128)(2,1)} async-done(((bf16[768,1536]{1,0:T(8,128)(2,1)}), bf16[192,1536]{1,0:T(8,128)(2,1)}) %reduce-scatter.15.cloned.1.call-update) | async-done | bytes 589840 | tf_op jit(solution)/shard_map/reduce_scatter | solution.py:250
  891.7 79.4 %all-reduce = (f32[2,384]{1,0:T(2,128)}, f32[1536]{0:T(1024)}, f32[2,768]{1,0:T(2,128)}, f32[4,768]{1,0:T(4,128)}) all-reduce(f32[2,384]{1,0:T(2,128)S(1)} %pad_maximum_fusion.6, f32[1536]{0:T(1024)} %get-tuple-element.355, f32[2,768]{1,0:T(2,128)S(1)} %pad_maximum_fusion.5, ...), channel_id=1, replica_groups=mesh['fsdp'=4,'context'=4,'tensor'=2] {'fsdp','context'}, use_global_device_ids=true, to_apply=%region_34.35 | all-reduce | flops 6912 | bytes 55296 | tf_op jit(solution)/shard_map/psum | solution.py:265
  973.6 21.2 %all-reduce.16.cloned.1.call-done = (bf16[3,192,384]{1,2,0:T(8,128)(2,1)}, bf16[384,192]{0,1:T(8,128)(2,1)}, bf16[192,1536]{1,0:T(8,128)(2,1)}, bf16[1536,192]{0,1:T(8,128)(2,1)}) async-done(((bf16[3,192,384]{1,2,0:T(8,128)(2,1)}, bf16[384,192]{0,1:T(8,128)(2,1)}, bf16[192,1536]{1,0:T(8,128)(2,1)}, bf16[1536,192]{0,1:T(8,128)(2,1)}), (bf16[3,192,384]{1,2,0:T(8,128)(2,1)}, bf16[384,192]{0,1:T(8,128)(2,1)}, ...) | async-done | bytes 1769488 | tf_op jit(solution)/shard_map/psum | solution.py:258
  (314 shorter events, 215.9 us)
Async XLA Ops:
  7.2 37.9 %all-gather.8.cloned.1.call-start = ((), (), s32[]{:S(2)}) async-start(), calls=%async_computation.6 | async-start | bytes 2211840 | tf_op jit(solution)/shard_map/all_gather | solution.py:78
  7.9 133.2 %all-gather.10.cloned.1.call-start = ((), (), s32[]{:S(2)}) async-start(), calls=%async_computation.7 | async-start | bytes 5898240 | tf_op jit(solution)/shard_map/all_gather | solution.py:94
  50.4 16.2 %copy-start.12 = (bf16[768,384]{0,1:T(8,128)(2,1)}, bf16[768,384]{0,1:T(8,128)(2,1)S(1)}, u32[]{:S(2)}) copy-start(bf16[768,384]{0,1:T(8,128)(2,1)S(1)} %fusion.81) | copy-start | bytes 1769476
  50.4 13.2 %copy-start.43 = (s32[3072]{0:T(1024)S(1)}, s32[3072]{0:T(1024)}, u32[]{:S(2)}) copy-start(s32[3072]{0:T(1024)} %param.27) | copy-start | bytes 36868
  51.6 233.3 %all-reduce.8.cloned.1.call-start = ((), (), s32[]{:S(2)}) async-start(), calls=%async_computation.8 | async-start | bytes 2359296 | tf_op jit(solution)/shard_map/psum | solution.py:135
  155.1 109.7 %copy-start.7 = (bf16[384,768]{0,1:T(8,128)(2,1)S(1)}, bf16[384,768]{0,1:T(8,128)(2,1)}, u32[]{:S(2)}) copy-start(bf16[384,768]{0,1:T(8,128)(2,1)} %all_gather.23) | copy-start | bytes 1769476
  155.1 5.0 copy-start.25
  155.1 5.0 copy-start.29
  173.1 4.9 copy-start.25
  173.1 4.9 copy-start.29
  191.0 4.9 copy-start.25
  191.0 4.9 copy-start.29
  208.9 4.9 copy-start.29
  226.8 4.9 copy-start.29
  244.7 4.9 copy-start.25
  244.7 4.9 copy-start.29
  264.8 20.1 %copy-start = (bf16[768,768]{1,0:T(8,128)(2,1)S(1)}, bf16[768,768]{1,0:T(8,128)(2,1)}, u32[]{:S(2)}) copy-start(bf16[768,768]{1,0:T(8,128)(2,1)} %param.16) | copy-start | bytes 3538948
  266.7 58.5 %all-gather.12.cloned.1.call-start = ((), (), s32[]{:S(2)}) async-start(), calls=%async_computation.9 | async-start | bytes 2949120 | tf_op jit(solution)/shard_map/all_gather | solution.py:80
  267.2 97.0 %all-gather.14.cloned.1.call-start = ((), (), s32[]{:S(2)}) async-start(), calls=%async_computation.10 | async-start | bytes 2949120 | tf_op jit(solution)/shard_map/all_gather | solution.py:81
  267.8 121.6 %all-reduce.10.cloned.1.call-start = ((), (), s32[]{:S(2)}) async-start(), calls=%async_computation.11 | async-start | bytes 2359296 | tf_op jit(solution)/shard_map/psum | solution.py:146
  267.9 246.0 %copy-start.32 = (f32[768]{0:T(1024)}, f32[768]{0:T(1024)S(1)}, u32[]{:S(2)}) copy-start(f32[768]{0:T(1024)S(1)} %get-tuple-element.277) | copy-start | bytes 9220
  268.0 121.5 %copy-start.37 = (f32[768]{0:T(1024)}, f32[768]{0:T(1024)S(1)}, u32[]{:S(2)}) copy-start(f32[768]{0:T(1024)S(1)} %get-tuple-element.273) | copy-start | bytes 9220
  268.0 246.0 %copy-start.26 = (f32[768]{0:T(1024)}, f32[768]{0:T(1024)S(1)}, u32[]{:S(2)}) copy-start(f32[768]{0:T(1024)S(1)} %get-tuple-element.274) | copy-start | bytes 9220
  284.9 40.3 %copy-start.47 = (f32[1536]{0:T(1024)S(1)}, f32[1536]{0:T(1024)}, u32[]{:S(2)}) copy-start(f32[1536]{0:T(1024)} %param.22) | copy-start | bytes 18436
  286.7 227.2 %copy-start.30 = (f32[768]{0:T(1024)}, f32[768]{0:T(1024)S(1)}, u32[]{:S(2)}) copy-start(f32[768]{0:T(1024)S(1)} %broadcast_multiply_fusion.5) | copy-start | bytes 9220
  287.4 226.6 %copy-start.34 = (f32[768]{0:T(1024)}, f32[768]{0:T(1024)S(1)}, u32[]{:S(2)}) copy-start(f32[768]{0:T(1024)S(1)} %add_rsqrt_fusion.1) | copy-start | bytes 9220
  369.6 72.6 %all-gather.18.cloned.1.call-start = ((), (), s32[]{:S(2)}) async-start(), calls=%async_computation.20 | async-start | bytes 2949120 | tf_op jit(solution)/shard_map/all_gather | solution.py:182
  371.9 120.7 %all-gather.16.cloned.1.call-start = ((), (), s32[]{:S(2)}) async-start(), calls=%async_computation.13 | async-start | bytes 2949120 | tf_op jit(solution)/shard_map/all_gather | solution.py:183
  372.6 141.3 %all-reduce.12.cloned.1.call-start = ((), (), s32[]{:S(2)}) async-start(), calls=%async_computation.12 | async-start | bytes 2359296 | tf_op jit(solution)/shard_map/psum | solution.py:164
  396.7 7.5 copy-start.3
  396.7 8.9 copy-start.45
  408.7 273.8 %reduce-scatter.9.cloned.1.call-start = ((), (), s32[]{:S(2)}) async-start(), calls=%async_computation.14 | async-start | bytes 2949120 | tf_op jit(solution)/shard_map/reduce_scatter | solution.py:221
  492.6 5.7 copy-start.23
  492.6 5.7 copy-start.36
  633.5 98.5 %reduce-scatter.11.cloned.1.call-start = ((), (), s32[]{:S(2)}) async-start(), calls=%async_computation.15 | async-start | bytes 2949120 | tf_op jit(solution)/shard_map/reduce_scatter | solution.py:224
  637.8 138.8 %reduce-scatter.19.cloned.1.call-start = ((), (), s32[]{:S(2)}) async-start(), calls=%async_computation.21 | async-start | bytes 2211840
  744.6 60.9 %reduce-scatter.13.cloned.1.call-start = ((), (), s32[]{:S(2)}) async-start(), calls=%async_computation.17 | async-start | bytes 737280 | tf_op jit(solution)/shard_map/reduce_scatter | solution.py:247
  747.4 98.4 %reduce-scatter.17.cloned.1.call-start = ((), (), s32[]{:S(2)}) async-start(), calls=%async_computation.19 | async-start | bytes 2949120 | tf_op jit(solution)/shard_map/reduce_scatter | solution.py:253
  753.3 132.8 %reduce-scatter.15.cloned.1.call-start = ((), (), s32[]{:S(2)}) async-start(), calls=%async_computation.18 | async-start | bytes 2949120 | tf_op jit(solution)/shard_map/reduce_scatter | solution.py:250
  759.9 211.2 %all-reduce.14.cloned.1.call-start = ((), (), s32[]{:S(2)}) async-start(), calls=%async_computation.16 | async-start | bytes 2359296 | tf_op jit(solution)/shard_map/psum | solution.py:241
  765.6 123.1 %copy-start.40 = (f32[768]{0:T(1024)S(1)}, f32[768]{0:T(1024)}, u32[]{:S(2)}) copy-start(f32[768]{0:T(1024)} %get-tuple-element.263) | copy-start | bytes 9220
  765.6 123.7 %copy-start.39 = (f32[768]{0:T(1024)S(1)}, f32[768]{0:T(1024)}, u32[]{:S(2)}) copy-start(f32[768]{0:T(1024)} %get-tuple-element.268) | copy-start | bytes 9220
  765.6 123.7 %copy-start.38 = (f32[768]{0:T(1024)S(1)}, f32[768]{0:T(1024)}, u32[]{:S(2)}) copy-start(f32[768]{0:T(1024)} %get-tuple-element.269) | copy-start | bytes 9220
  765.6 123.7 %copy-start.41 = (f32[768]{0:T(1024)S(1)}, f32[768]{0:T(1024)}, u32[]{:S(2)}) copy-start(f32[768]{0:T(1024)} %get-tuple-element.338) | copy-start | bytes 9220
  765.6 124.3 %copy-start.11 = (bf16[6,768,64]{1,2,0:T(8,128)(2,1)S(1)}, bf16[6,768,64]{1,2,0:T(8,128)(2,1)}, u32[]{:S(2)}) copy-start(bf16[6,768,64]{1,2,0:T(8,128)(2,1)} %get-tuple-element.116) | copy-start | bytes 1769476
  765.6 229.2 %all-reduce.16.cloned.1.call-start = ((), (), s32[]{:S(2)}) async-start(), calls=%async_computation.22 | async-start | bytes 3833856 | tf_op jit(solution)/shard_map/psum | solution.py:258
  779.3 112.2 %copy-start.21 = (bf16[768,384]{1,0:T(8,128)(2,1)S(1)}, bf16[768,384]{1,0:T(8,128)(2,1)}, u32[]{:S(2)}) copy-start(bf16[768,384]{1,0:T(8,128)(2,1)} %reduce-scatter.11.cloned.1.call-done) | copy-start | bytes 1769476
  994.8 6.1 copy-start.19
  (39 other events, 94.2 us)
Sparse Core Ops, SparseCore 0:
  9.8 35.1 all-gather.7
  51.7 89.3 all-gather.9
  266.8 18.0 all-reduce.7
  286.6 38.5 all-gather.11
  326.8 37.3 all-gather.13
  369.8 19.6 all-reduce.9
  391.0 51.1 all-gather.17
  443.8 48.7 all-gather.15
  495.5 18.4 all-reduce.11
  633.6 48.8 reduce-scatter.8
  684.8 47.0 reduce-scatter.10
  744.7 31.8 reduce-scatter.18
  780.0 25.4 reduce-scatter.12
  808.4 37.3 reduce-scatter.16
  848.7 37.3 reduce-scatter.14
  888.9 19.6 all-reduce.13
  911.6 83.1 all-reduce.15
